TPU v7x, 32 devices: a whole 2x2x4 slice. The times are simulated.
32 devices in a mesh: tm: 8 (over z, x), rows: 4 (over y, core).
Axes of the slice: x: 2, y: 2, z: 4, core: 2. Of those that a mesh axis runs over, the one named last changes fastest.
Arguments:
- slc_stack: bfloat16 [32, 2, 32, 2048], P('tm', None, 'rows'), may hold values from -6 to 6
- partner_count: int32 [32], P('tm'), may hold values from 2 to 6, as said below
- look_sizes: int32 [32, 2], P('tm'), may hold values from 1 to 8, as said below
Outputs:
- interferogram: bfloat16 [32, 6, 2, 32, 2048], P('tm', None, None, 'rows')
- coherence: bfloat16 [32, 6, 32, 2048], P('tm', None, 'rows')
Inputs may be any that keep to these rules, and one draw needn't show every extreme that they name: `partner_count`: some acquisition has 6 partners and some has 2. `look_sizes`: Half-heights run from 1 to 2, half-widths from 2 to 8; some acquisition has (2, 8) and some (1, 2).
All inputs are finite; a program needn't handle non-finite values.
Results may differ from a plain program's by a relative error of at most 0.0049.
Values may be sent and summed in bfloat16 or wider, within the bound.
A program may use at most 64 MiB of HBM per device.

v0:
```python
import functools

import jax
import jax.numpy as jnp
from jax import lax
from jax.experimental import pallas as pl
from jax.experimental.pallas import tpu as pltpu
from jax.sharding import PartitionSpec as P

MAXP = 6
HR = 2
LANES = 128
BLOCK = 256

epsilon = 1e-06
MESH = pl.DeviceIdType.MESH


def kernel(
    acq_total, counts_in, looks_in, x, ifg, coh,
    held, planes, power, sums, wide, bands, own_box, counts, looks,
    send_sem, recv_sem, table_sem,
):
    tm, line = lax.axis_index("tm"), lax.axis_index("rows")
    tm_count, line_count = lax.axis_size("tm"), lax.axis_size("rows")
    per_dev, _, rows = x.shape[:3]
    total = held.shape[0]
    far = MAXP - per_dev
    even = lax.rem(tm, 2) == 0
    odd = lax.rem(tm, 2) == 1
    steps = [
        (tm >= 1, {"tm": tm - 1}),
        (tm >= 2, {"tm": tm - 2}),
        (tm + 1 < tm_count, {"tm": tm + 1}),
        (tm + 2 < tm_count, {"tm": tm + 2}),
        (line >= 1, {"rows": line - 1}),
        (line + 1 < line_count, {"rows": line + 1}),
    ]
    tables = [
        pltpu.make_async_copy(counts_in, counts, table_sem.at[0]),
        pltpu.make_async_copy(looks_in, looks, table_sem.at[1]),
    ]
    for table in tables:
        table.start()
    barrier = pltpu.get_barrier_semaphore()
    for there, device in steps:

        @pl.when(there)
        def _():
            pl.semaphore_signal(barrier, inc=1, device_id=device, device_id_type=MESH)

    pl.semaphore_wait(barrier, sum(jnp.where(there, 1, 0) for there, _ in steps))

    near_dev, far_dev, next_dev = {"tm": tm - 1}, {"tm": tm - 2}, {"tm": tm + 1}
    starts = [per_dev, per_dev + far, 2 * per_dev]
    sizes = [far, per_dev - far, far]
    sides = [(0, HR), (rows - HR, rows)]
    mid_slot = 6
    down_slot = mid_slot + MAXP
    up_slot = down_slot + 3
    own_slot = up_slot + 3
    onward_slot = own_slot + 2

    def copy(src, dst, send, recv, device):
        return pltpu.make_async_remote_copy(
            src_ref=src,
            dst_ref=dst,
            send_sem=send_sem.at[send],
            recv_sem=recv_sem.at[recv],
            device_id=device,
            device_id_type=MESH,
        )

    def span(g, low, high):
        return held.at[pl.ds(starts[g], sizes[g]), :, pl.ds(HR + low, high - low)]

    def edge(g, side, device):
        low, high = sides[side]
        src = x.at[pl.ds(starts[g] % per_dev, sizes[g]), :, pl.ds(low, high - low)]
        return copy(src, span(g, low, high), 2 * g + side, 2 * g + side, device)

    def middle(p, device):
        src = x.at[p % per_dev, :, pl.ds(HR, rows - 2 * HR)]
        dst = held.at[p, :, pl.ds(2 * HR, rows - 2 * HR)]
        slot_at = mid_slot + p - per_dev
        return copy(src, dst, slot_at, slot_at, device)

    def onward_edge(side):
        low, high = sides[side]
        return copy(span(2, low, high), span(0, low, high), onward_slot + side, side, next_dev)

    def onward_middle(k):
        src = held.at[2 * per_dev + k, :, pl.ds(2 * HR, rows - 2 * HR)]
        dst = held.at[per_dev + k, :, pl.ds(2 * HR, rows - 2 * HR)]
        return copy(src, dst, onward_slot + 2 + k, mid_slot + k, next_dev)

    def down(g):
        src, dst = span(g, rows - HR, rows), span(g, -HR, 0)
        return copy(src, dst, down_slot + g, down_slot + g, {"rows": line + 1})

    def up(g):
        src, dst = span(g, 0, HR), span(g, rows, rows + HR)
        return copy(src, dst, up_slot + g, up_slot + g, {"rows": line - 1})

    def own_down():
        src = x.at[:, :, pl.ds(rows - HR, HR)]
        dst = held.at[pl.ds(0, per_dev), :, pl.ds(0, HR)]
        return copy(src, dst, own_slot, own_slot, {"rows": line + 1})

    def own_up():
        src = x.at[:, :, pl.ds(0, HR)]
        dst = held.at[pl.ds(0, per_dev), :, pl.ds(HR + rows, HR)]
        return copy(src, dst, own_slot + 1, own_slot + 1, {"rows": line - 1})

    below, above = line + 1 < line_count, line >= 1
    has = [tm + 1 < tm_count, tm + 1 < tm_count, tm + 2 < tm_count]
    passes = even & has[2]
    sends = [odd, tm >= 1, tm >= 2]
    to = [near_dev, near_dev, far_dev]

    @pl.when(below)
    def _():
        own_down().start()

    @pl.when(above)
    def _():
        own_up().start()

    for g in (2, 1, 0):

        @pl.when(sends[g])
        def _():
            for side in range(2):
                edge(g, side, to[g]).start()

    for g in (2, 1, 0):

        @pl.when(sends[g])
        def _():
            for k in range(sizes[g]):
                middle(starts[g] + k, to[g]).start()

    ext_rows, tiles = held.shape[2], held.shape[3]
    blocks = tiles * LANES // BLOCK
    depth = wide.shape[1]

    def outer(a):
        return jnp.where(looks[0, a] >= HR, 1.0, 0.0).astype(jnp.float32)

    def place(p, r, get):
        parts = [get(part).astype(jnp.float32) for part in range(2)]
        outside = line == 0 if r < HR else line == line_count - 1 if r >= HR + rows else None
        if outside is not None:
            parts = [jnp.where(outside, 0.0, part) for part in parts]
        planes[p, 0, r] = parts[0]
        planes[p, 1, r] = parts[1]
        power[p, r] = parts[0] * parts[0] + parts[1] * parts[1]

    def row_window(get, field, edge_weight):
        for h in range(0, tiles, 8):
            v = get(h)
            pairs = [v[r] + v[r + 1] for r in range(1, rows + 2)]
            for r in range(rows):
                total_row = pairs[r] + v[r + 3] + (v[r] + v[r + 4]) * edge_weight
                sums[field, pl.ds(h * rows + r, 8, stride=rows), :] = total_row

    def box(a, count):
        for t in range(tiles):
            m, side = (t + 1) // 2, (t + 1) % 2
            for f in range(0, count, 2):
                pieces = [
                    sums[g, t * rows : (t + 1) * rows, :] for g in range(f, min(f + 2, count))
                ]
                piece = jnp.concatenate(pieces, 0).astype(jnp.bfloat16)
                at = slice(f * rows, f * rows + len(pieces) * rows)
                wide[m, at, side * LANES : (side + 1) * LANES] = piece
        lead = wide[0:blocks].reshape(blocks * depth, BLOCK)
        tail = wide[1 : blocks + 1].reshape(blocks * depth, BLOCK)
        result = jnp.dot(lead, bands[a, 0], preferred_element_type=jnp.float32)
        result = result + jnp.dot(tail, bands[a, 1], preferred_element_type=jnp.float32)
        return result.reshape(blocks, depth, BLOCK)

    def slot(a, p):
        weight = outer(a)

        def row(q, part, r, h):
            return planes[q, part, r, h : h + 8, :]

        def real_part(h):
            return [
                row(a, 0, r, h) * row(p, 0, r, h) + row(a, 1, r, h) * row(p, 1, r, h)
                for r in range(ext_rows)
            ]

        def imag_part(h):
            return [
                row(a, 1, r, h) * row(p, 0, r, h) - row(a, 0, r, h) * row(p, 1, r, h)
                for r in range(ext_rows)
            ]

        def partner_power(h):
            return [power[p, r, h : h + 8, :] for r in range(ext_rows)]

        row_window(real_part, 0, weight)
        row_window(imag_part, 1, weight)
        row_window(partner_power, 2, weight)
        boxed = box(a, 3)
        j = p - a - 1
        live = (j < counts[a]) & (tm * per_dev + p < acq_total)
        area = ((2 * looks[0, a] + 1) * (2 * looks[1, a] + 1)).astype(jnp.float32)
        scale = 1.0 / jnp.full((rows, BLOCK), area, jnp.float32)
        for n in range(blocks):
            own = own_box[a, n]
            real, imag, other = [boxed[n, f * rows : (f + 1) * rows, :] for f in range(3)]
            magnitude = jnp.sqrt(real * real + imag * imag)
            value = magnitude * lax.rsqrt(own * other + epsilon)
            where = slice(n * BLOCK, (n + 1) * BLOCK)
            ifg[a, j, 0, :, where] = jnp.where(live, real * scale, 0.0).astype(ifg.dtype)
            ifg[a, j, 1, :, where] = jnp.where(live, imag * scale, 0.0).astype(ifg.dtype)
            coh[a, j, :, where] = jnp.where(live, value, 0.0).astype(coh.dtype)

    def relay(g):
        @pl.when(has[g])
        def _():
            for side in range(2):
                edge(g, side, to[g]).wait_recv()

        if g == 2:

            @pl.when(passes)
            def _():
                for side in range(2):
                    onward_edge(side).start()

        @pl.when(has[g] & below)
        def _():
            down(g).start()

        @pl.when(has[g] & above)
        def _():
            up(g).start()

    def halo(g):
        @pl.when(has[g] & below)
        def _():
            up(g).wait_recv()

        @pl.when(has[g] & above)
        def _():
            down(g).wait_recv()

    zero = jnp.zeros((depth, LANES), wide.dtype)
    wide[0, :, :LANES] = zero
    wide[blocks, :, LANES:] = zero
    inner = lax.broadcasted_iota(jnp.int32, (BLOCK, BLOCK), 0)
    across = lax.broadcasted_iota(jnp.int32, (BLOCK, BLOCK), 1)

    for table in tables:
        table.wait()

    @pl.loop(0, per_dev)
    def _(a):
        reach = looks[1, a]
        bands[a, 0] = jnp.where(jnp.abs(inner - LANES - across) <= reach, 1.0, 0.0).astype(
            jnp.bfloat16
        )
        bands[a, 1] = jnp.where(jnp.abs(inner + LANES - across) <= reach, 1.0, 0.0).astype(
            jnp.bfloat16
        )
        for r in range(rows):
            place(a, HR + r, lambda part: x[a, part, r])

    relay(2)
    relay(1)

    @pl.when(line >= 1)
    def _():
        own_down().wait_recv()

    @pl.when(line + 1 < line_count)
    def _():
        own_up().wait_recv()

    @pl.loop(0, per_dev)
    def _(a):
        for r in list(range(HR)) + list(range(HR + rows, ext_rows)):
            place(a, r, lambda part: held[a, part, r])
        weight = outer(a)
        row_window(lambda h: [power[a, r, h : h + 8, :] for r in range(ext_rows)], 0, weight)
        own_box[a] = box(a, 1)[:, :rows, :]

    @pl.when(has[2])
    def _():
        for k in range(far):
            middle(2 * per_dev + k, far_dev).wait_recv()

    @pl.when(passes)
    def _():
        for k in range(far):
            onward_middle(k).start()

    relay(0)

    @pl.loop(0, per_dev - 1)
    def _(a):
        @pl.loop(a + 1, per_dev)
        def _(p):
            slot(a, p)

    order = [2 * per_dev + k for k in range(far)]
    order += [per_dev + k for k in range(far, per_dev)] + [per_dev + k for k in range(far)]

    for p in order:
        g = 2 if p >= starts[2] else 1 if p >= starts[1] else 0
        if g < 2:

            @pl.when(has[g])
            def _():
                middle(p, to[g]).wait_recv()

        if p == starts[g]:
            halo(g)

        for r in range(ext_rows):
            place(p, r, lambda part: held[p, part, r])

        @pl.loop(max(0, p - MAXP), per_dev)
        def _(a):
            slot(a, p)

    @pl.when(above)
    def _():
        own_up().wait_send()

    @pl.when(below)
    def _():
        own_down().wait_send()

    for g in range(3):

        @pl.when(has[g] & below)
        def _():
            down(g).wait_send()

        @pl.when(has[g] & above)
        def _():
            up(g).wait_send()

        @pl.when(sends[g])
        def _():
            for side in range(2):
                edge(g, side, to[g]).wait_send()
            for k in range(sizes[g]):
                middle(starts[g] + k, to[g]).wait_send()

    @pl.when(passes)
    def _():
        for side in range(2):
            onward_edge(side).wait_send()
        for k in range(far):
            onward_middle(k).wait_send()


def computed(x, counts, looks, acq_total):
    per_dev, parts, rows, tiles, lanes = x.shape
    total, ext_rows = per_dev + MAXP, rows + 2 * HR
    cols = tiles * lanes
    blocks = cols // BLOCK
    slots = 16 + 2 * MAXP
    hbm, vmem = [pl.BlockSpec(memory_space=space) for space in (pltpu.HBM, pltpu.VMEM)]
    return pl.pallas_call(
        functools.partial(kernel, acq_total),
        in_specs=[hbm, hbm, vmem],
        out_specs=[vmem, vmem],
        out_shape=[
            jax.ShapeDtypeStruct((per_dev, MAXP, 2, rows, cols), jnp.bfloat16),
            jax.ShapeDtypeStruct((per_dev, MAXP, rows, cols), jnp.bfloat16),
        ],
        scratch_shapes=[
            pltpu.VMEM((total, parts, ext_rows, tiles, lanes), x.dtype),
            pltpu.VMEM((total, parts, ext_rows, tiles, lanes), jnp.float32),
            pltpu.VMEM((total, ext_rows, tiles, lanes), jnp.float32),
            pltpu.VMEM((3, tiles * rows, lanes), jnp.float32),
            pltpu.VMEM((blocks + 1, 4 * rows, BLOCK), jnp.bfloat16),
            pltpu.VMEM((per_dev, 2, BLOCK, BLOCK), jnp.bfloat16),
            pltpu.VMEM((per_dev, blocks, rows, BLOCK), jnp.float32),
            pltpu.SMEM((per_dev,), jnp.int32),
            pltpu.SMEM((2, per_dev), jnp.int32),
            pltpu.SemaphoreType.DMA((slots,)),
            pltpu.SemaphoreType.DMA((slots,)),
            pltpu.SemaphoreType.DMA((2,)),
        ],
        compiler_params=pltpu.CompilerParams(
            collective_id=0, has_side_effects=True, vmem_limit_bytes=40 * 1024 * 1024
        ),
        name="insar_boxes",
    )(*[pltpu.with_memory_space_constraint(table, pltpu.HBM) for table in (counts, looks)], x)


def local(slc_stack, partner_count, look_sizes):
    tiled = slc_stack.reshape(slc_stack.shape[:-1] + (-1, LANES))
    acq_total = lax.axis_size("tm") * slc_stack.shape[0]
    return tuple(computed(tiled, partner_count, look_sizes.T, acq_total))


def solution(mesh):
    return jax.shard_map(
        local,
        mesh=mesh,
        in_specs=(P("tm", None, "rows", None), P("tm"), P("tm", None)),
        out_specs=(P("tm", None, None, "rows", None), P("tm", None, "rows", None)),
        check_vma=False,
    )
```

profile of v0, /device:TPU:0, one launch (start us, length us, event | category | flops | bytes accessed | tf_op | source)
XLA Modules:
  0.0 21.7 jit_solution(7661688934115273340)
XLA Ops:
  0.6 1.0 %copy.5 = bf16[8,8,16,128]{3,2,1,0:T(8,128)(2,1)S(1)} copy(bf16[8,8,16,128]{3,1,2,0:T(8,128)(2,1)} %bitcast.7) | data formatting | bytes 524288
  1.6 18.0 %insar_boxes.1 = (bf16[4,6,2,8,2048]{4,3,2,1,0:T(8,128)(2,1)S(1)}, bf16[4,6,8,2048]{3,2,1,0:T(8,128)(2,1)S(1)}) custom-call(s32[4]{0:T(128)} %counts_in.1, s32[2,4]{1,0:T(2,128)} %bitcast.8, bf16[4,2,8,16,128]{4,3,2,1,0:T(8,128)(2,1)S(1)} %bitcast.6), custom_call_target="tpu_custom_call" | custom-call | tf_op jit(solution)/shard_map/insar_boxes/pallas_call | solution.py:371
  19.7 1.1 %copy.8 = bf16[4,6,2,8,2048]{4,3,2,1,0:T(8,128)(2,1)} copy(bf16[4,6,2,8,2048]{4,3,2,1,0:T(8,128)(2,1)S(1)} %get-tuple-element.4) | data formatting | bytes 3145728
  20.8 0.9 %copy.9 = bf16[4,6,8,2048]{3,2,1,0:T(8,128)(2,1)} copy(bf16[4,6,8,2048]{3,2,1,0:T(8,128)(2,1)S(1)} %get-tuple-element.5) | data formatting | bytes 1572864
where the time goes:
time: 21.8 us; the launch traced here: 21.7 us
  Pallas kernels  18 us (83%)
  local copies, waits for them, and re-layouts  3.01 us (14%)
  between operations  0.65 us (3%)
    pallas_call x1, Pallas kernels, computed(): pl.pallas_call(functools.partial(kernel, acq_total), in_specs=[hbm, hbm,...  18 us
    unnamed x3, local copies, waits for them, and re-layouts  3.01 us

commit v1 on v0

v1 whole, which is shorter than its diff:
```python
import functools
import itertools

import jax
import jax.numpy as jnp
from jax import lax
from jax.experimental import pallas as pl
from jax.experimental.pallas import tpu as pltpu
from jax.sharding import PartitionSpec as P

MAXP = 6
HR = 2
LANES = 128

epsilon = 1e-06
tiny = 1.2e-38
MESH = pl.DeviceIdType.MESH


class Pieces:
    def __init__(self, src, dst, send, recv, device):
        self.src, self.dst, self.send, self.recv, self.device = src, dst, send, recv, device

    def over(self, *at):
        return pltpu.make_async_remote_copy(
            src_ref=self.src.at[at] if at else self.src,
            dst_ref=self.dst.at[at] if at else self.dst,
            send_sem=self.send,
            recv_sem=self.recv,
            device_id=self.device,
            device_id_type=MESH,
        )

    def start(self):
        for at in itertools.product(*[range(size) for size in self.src.shape[:-2]]):
            self.over(*at).start()

    def wait_send(self):
        self.over().wait_send()

    def wait_recv(self):
        self.over().wait_recv()


def kernel(
    acq_total, counts_in, looks_in, x, ifg, coh,
    held, planes, power, sums_a, sums_b, lhs_a, lhs_b, bands, own_box, counts, looks,
    send_sem, recv_sem, local_sem, ready_sem,
):
    tm, line = lax.axis_index("tm"), lax.axis_index("rows")
    tm_count, line_count = lax.axis_size("tm"), lax.axis_size("rows")
    per_dev, _, rows, cols = x.shape
    total = held.shape[0]
    tiles = cols // LANES
    half = tiles // 2
    far = MAXP - per_dev
    ext_rows = rows + 2 * HR
    even = lax.rem(tm, 2) == 0
    odd = lax.rem(tm, 2) == 1
    below, above = line + 1 < line_count, line >= 1
    near_dev, far_dev, next_dev = {"tm": tm - 1}, {"tm": tm - 2}, {"tm": tm + 1}
    down_dev, up_dev = {"rows": line + 1}, {"rows": line - 1}

    local_copies = [
        pltpu.make_async_copy(x, held.at[pl.ds(0, per_dev), :, pl.ds(0, rows)], local_sem.at[0]),
        pltpu.make_async_copy(counts_in, counts, local_sem.at[1]),
        pltpu.make_async_copy(looks_in, looks, local_sem.at[2]),
    ]

    barrier = pltpu.get_barrier_semaphore()
    for there, device in [
        (tm + 1 < tm_count, next_dev),
        (tm + 2 < tm_count, {"tm": tm + 2}),
        (below, down_dev),
    ]:

        @pl.when(there)
        def _():
            pl.semaphore_signal(barrier, inc=1, device_id=device, device_id_type=MESH)

    earlier = sum(jnp.where(there, 1, 0) for there in (tm >= 1, tm >= 2, above))

    @pl.when(earlier > 0)
    def _():
        pl.semaphore_wait(barrier, earlier)

    for index, (there, device) in enumerate([(above, up_dev), (odd, near_dev)]):

        @pl.when(there)
        def _():
            pl.semaphore_signal(
                ready_sem.at[index], inc=1, device_id=device, device_id_type=MESH
            )

    starts = [per_dev, per_dev + far, 2 * per_dev]
    sizes = [far, per_dev - far, far]
    sides = [0, rows - HR]
    mid_slot = 6
    down_slot = mid_slot + MAXP
    up_slot = down_slot + 3
    own_slot = up_slot + 3
    onward_slot = own_slot + 2
    def copy(src, dst, send, recv, device):
        return Pieces(src, dst, send_sem.at[send], recv_sem.at[recv], device)

    def span(g, low, size):
        return held.at[pl.ds(starts[g], sizes[g]), :, pl.ds(low, size)]

    def edge(g, side, device):
        src = x.at[pl.ds(starts[g] % per_dev, sizes[g]), :, pl.ds(sides[side], HR)]
        return copy(src, span(g, sides[side], HR), 2 * g + side, 2 * g + side, device)

    def middle(p, device):
        src = x.at[p % per_dev, :, pl.ds(HR, rows - 2 * HR)]
        dst = held.at[p, :, pl.ds(HR, rows - 2 * HR)]
        at = mid_slot + p - per_dev
        return copy(src, dst, at, at, device)

    def onward_edge(side):
        low = sides[side]
        return copy(span(2, low, HR), span(0, low, HR), onward_slot + side, side, next_dev)

    def onward_middle(k):
        src = held.at[2 * per_dev + k, :, pl.ds(HR, rows - 2 * HR)]
        dst = held.at[per_dev + k, :, pl.ds(HR, rows - 2 * HR)]
        return copy(src, dst, onward_slot + 2 + k, mid_slot + k, next_dev)

    def down(g):
        return copy(span(g, rows - HR, HR), span(g, rows, HR), down_slot + g, down_slot + g, down_dev)

    def up(g):
        return copy(span(g, 0, HR), span(g, rows + HR, HR), up_slot + g, up_slot + g, up_dev)

    def own_down():
        src = x.at[:, :, pl.ds(rows - HR, HR)]
        dst = held.at[pl.ds(0, per_dev), :, pl.ds(rows, HR)]
        return copy(src, dst, own_slot, own_slot, down_dev)

    def own_up():
        src = x.at[:, :, pl.ds(0, HR)]
        dst = held.at[pl.ds(0, per_dev), :, pl.ds(rows + HR, HR)]
        return copy(src, dst, own_slot + 1, own_slot + 1, up_dev)

    has = [tm + 1 < tm_count, tm + 1 < tm_count, tm + 2 < tm_count]
    passes = even & has[2]
    sends = [odd, tm >= 1, tm >= 2]
    to = [near_dev, near_dev, far_dev]

    def when(condition, action):
        @pl.when(condition)
        def _():
            action()

    def send_edges(g):
        for side in range(2):
            edge(g, side, to[g]).start()

    def send_middles(g):
        for k in range(sizes[g]):
            middle(starts[g] + k, to[g]).start()

    when(above, lambda: own_up().start())
    for g in (2, 0, 1):
        when(sends[g], lambda: send_edges(g))
    for g in (2, 0, 1):
        when(sends[g], lambda: send_middles(g))
    for local_copy in local_copies:
        local_copy.start()

    def relay(g):
        def act():
            for side in range(2):
                edge(g, side, to[g]).wait_recv()
            when(below, lambda: down(g).start())
            when(above, lambda: up(g).start())

        when(has[g], act)

    def halo(g):
        when(has[g] & below, lambda: up(g).wait_recv())
        when(has[g] & above, lambda: down(g).wait_recv())

    def place(p, first, count, keep):
        for part in range(2):
            for t in range(tiles):
                lanes = slice(t * LANES, (t + 1) * LANES)
                v = held[p, part, first : first + count, lanes].astype(jnp.float32)
                if keep is not None:
                    v = jnp.where(keep, v, 0.0)
                planes[p, part, pl.ds(first * tiles + t, count, stride=tiles), :] = v

    order = [rows + k for k in range(HR)] + list(range(rows)) + [rows + HR + k for k in range(HR)]

    def plane(p, part, r, h):
        at = order[r] * tiles + h
        return planes[p, part, at : at + 8, :]

    side_row = lax.broadcasted_iota(jnp.int32, (2 * HR, LANES), 0)
    inside = ((side_row < HR) & above) | ((side_row >= HR) & below)
    near_edge = lax.broadcasted_iota(jnp.int32, (2 * rows, LANES), 1) < LANES // 2
    zero = jnp.zeros((rows, LANES), jnp.float32)

    def spread(get, count, out):
        pieces = [get(t) for t in range(-1, count + 1)]
        for t in range(0, count, 2):
            at = slice(t * rows, (t + 2) * rows)
            out[at, :LANES] = pieces[t + 1]
            out[at, LANES : 2 * LANES] = pieces[t + 2]
            out[at, 2 * LANES :] = jnp.where(near_edge, pieces[t + 3], pieces[t])

    def pair(first, second):
        return jnp.concatenate([first, second], 0).astype(jnp.bfloat16)

    def partner_power(p):
        for h in range(0, tiles, 8):
            v = []
            for r in range(ext_rows):
                re, im = plane(p, 0, r, h), plane(p, 1, r, h)
                v.append(re * re + im * im)
            pairs = [v[r] + v[r + 1] for r in range(1, rows + 2)]
            for r in range(rows):
                short = pairs[r] + v[r + 3]
                where = pl.ds(h * rows + r, 8, stride=rows)
                sums_a[0, where, :] = short
                sums_a[1, where, :] = short + (v[r] + v[r + 4])
        for n in range(2):

            def tile(t):
                return sums_a[n, t * rows : (t + 1) * rows, :] if 0 <= t < tiles else zero

            spread(lambda t: pair(tile(t), tile(t + half)), half, power.at[p, n])

    def boxed_power(a, p):
        result = jnp.dot(power[p, jnp.where(looks[0, a] >= HR, 1, 0)], bands[a], preferred_element_type=jnp.float32)
        result = result.reshape(half // 2, 2, rows, 2 * LANES)
        return [result[m % (half // 2), m // (half // 2)] for m in range(half)]

    def first_half(a, p, sums, lhs):
        outer = jnp.where(looks[0, a] >= HR, 1.0, 0.0).astype(jnp.float32)
        for h in range(0, tiles, 8):
            real, imag = [], []
            for r in range(ext_rows):
                own_re, own_im = plane(a, 0, r, h), plane(a, 1, r, h)
                far_re, far_im = plane(p, 0, r, h), plane(p, 1, r, h)
                real.append(own_re * far_re + own_im * far_im)
                imag.append(own_im * far_re - own_re * far_im)
            for field, v in enumerate((real, imag)):
                pairs = [v[r] + v[r + 1] for r in range(1, rows + 2)]
                for r in range(rows):
                    row_total = pairs[r] + v[r + 3] + (v[r] + v[r + 4]) * outer
                    sums[field, pl.ds(h * rows + r, 8, stride=rows), :] = row_total

        def fields(t):
            if not 0 <= t < tiles:
                return pair(zero, zero)
            return pair(*[sums[f, t * rows : (t + 1) * rows, :] for f in range(2)])

        spread(fields, tiles, lhs)

    def store(ref, at, value):
        for side in range(2):
            where = slice(at + side * LANES, at + (side + 1) * LANES)
            ref[:, where] = value[side * rows : (side + 1) * rows]

    def second_half(a, p, lhs):
        j = p - a - 1
        live = (j < counts[a]) & (tm * per_dev + p < acq_total)
        which = jnp.where(live, a, per_dev)
        boxed = jnp.dot(lhs[...], bands[which], preferred_element_type=jnp.float32)
        boxed = boxed.reshape(half, 2, rows, 2 * LANES)
        other = boxed_power(a, p)
        area = ((2 * looks[0, a] + 1) * (2 * looks[1, a] + 1)).astype(jnp.float32)
        scale = 1.0 / jnp.full((rows, 2 * LANES), area, jnp.float32)
        for m in range(half):
            re, im = boxed[m, 0], boxed[m, 1]
            size = re * re + im * im
            level = own_box[a, m] * other[m] + epsilon
            value = size * lax.rsqrt(jnp.maximum(size * level, tiny))
            for ref, v in ((ifg.at[a, j, 0], re * scale), (ifg.at[a, j, 1], im * scale), (coh.at[a, j], value)):
                store(ref, 2 * m * LANES, pair(v[:, :LANES], v[:, LANES:]))

    def slot(a, p, sums, lhs):
        first_half(a, p, sums, lhs)
        second_half(a, p, lhs)

    scratch = [(sums_a, lhs_a), (sums_b, lhs_b)]

    def slots(pairs):
        for n, (a, p) in enumerate(pairs):
            slot(a, p, *scratch[n % 2])

    for local_copy in local_copies:
        local_copy.wait()

    inner = lax.broadcasted_iota(jnp.int32, (3 * LANES, 2 * LANES), 0)
    across = lax.broadcasted_iota(jnp.int32, (3 * LANES, 2 * LANES), 1)
    source = jnp.where(inner < 2 * LANES + LANES // 2, inner, inner - 3 * LANES)
    distance = jnp.abs(source - across)
    bands[per_dev] = jnp.zeros((3 * LANES, 2 * LANES), jnp.bfloat16)

    @pl.loop(0, per_dev)
    def _(a):
        bands[a] = jnp.where(distance <= looks[1, a], 1.0, 0.0).astype(jnp.bfloat16)
        place(a, 0, rows, None)

    @pl.when(below)
    def _():
        pl.semaphore_wait(ready_sem.at[0], 1)
        own_down().start()

    @pl.when(even)
    def _():
        pl.semaphore_wait(ready_sem.at[1], 1)

    when(above, lambda: own_down().wait_recv())
    when(below, lambda: own_up().wait_recv())

    @pl.loop(0, per_dev)
    def _(a):
        place(a, rows, 2 * HR, inside)
        partner_power(a)
        box = boxed_power(a, a)
        for m in range(half):
            own_box[a, m] = box[m]

    own_pairs = [(a, p) for p in range(1, per_dev) for a in range(p)]
    early, late = own_pairs[: len(own_pairs) // 2], own_pairs[len(own_pairs) // 2 :]

    relay(2)

    @pl.when(passes)
    def _():
        for side in range(2):
            onward_edge(side).start()

    when(even, lambda: relay(0))
    slots(early)
    relay(1)
    slots(late)

    @pl.when(has[2])
    def _():
        for k in range(far):
            middle(2 * per_dev + k, far_dev).wait_recv()
            when(passes, lambda: onward_middle(k).start())

    when(odd, lambda: relay(0))

    def partner(p, there, first):
        place(p, 0, rows, there)
        place(p, rows, 2 * HR, inside & there)
        partner_power(p)
        slots([(a, p) for a in range(first, per_dev)])

    halo(2)
    for k in range(far):
        partner(2 * per_dev + k, has[2], 2 * per_dev + k - MAXP)

    def arrived(p):
        g = 0 if p < starts[1] else 1
        when(has[g], lambda: middle(p, to[g]).wait_recv())
        if p == starts[g]:
            halo(g)

    turns = list(range(starts[0], starts[2]))
    for p_even, p_odd in zip(turns, turns[far:] + turns[:far]):
        when(even, lambda: arrived(p_even))
        when(odd, lambda: arrived(p_odd))
        partner(jnp.where(odd, p_odd, p_even), has[0], 0)

    when(above, lambda: own_up().wait_send())
    when(below, lambda: own_down().wait_send())
    for g in range(3):
        when(has[g] & below, lambda: down(g).wait_send())
        when(has[g] & above, lambda: up(g).wait_send())

        @pl.when(sends[g])
        def _():
            for side in range(2):
                edge(g, side, to[g]).wait_send()
            for k in range(sizes[g]):
                middle(starts[g] + k, to[g]).wait_send()

    @pl.when(passes)
    def _():
        for side in range(2):
            onward_edge(side).wait_send()
        for k in range(far):
            onward_middle(k).wait_send()


def computed(x, counts, looks, acq_total):
    per_dev, parts, rows, cols = x.shape
    total, ext_rows = per_dev + MAXP, rows + 2 * HR
    tiles = cols // LANES
    slots = 16 + 2 * MAXP
    spare = max(0, 2 * per_dev - 1 - MAXP)
    hbm, vmem = [pl.BlockSpec(memory_space=space) for space in (pltpu.HBM, pltpu.VMEM)]
    return pl.pallas_call(
        functools.partial(kernel, acq_total),
        in_specs=[hbm, hbm, hbm],
        out_specs=[vmem, vmem],
        out_shape=[
            jax.ShapeDtypeStruct((per_dev, MAXP + spare, 2, rows, cols), jnp.bfloat16),
            jax.ShapeDtypeStruct((per_dev, MAXP + spare, rows, cols), jnp.bfloat16),
        ],
        scratch_shapes=[
            pltpu.VMEM((total, parts, 2 * rows, cols), x.dtype),
            pltpu.VMEM((total, parts, ext_rows * tiles, LANES), jnp.float32),
            pltpu.VMEM((total, 2, tiles // 2 * rows, 3 * LANES), jnp.bfloat16),
            pltpu.VMEM((2, tiles * rows, LANES), jnp.float32),
            pltpu.VMEM((2, tiles * rows, LANES), jnp.float32),
            pltpu.VMEM((tiles * rows, 3 * LANES), jnp.bfloat16),
            pltpu.VMEM((tiles * rows, 3 * LANES), jnp.bfloat16),
            pltpu.VMEM((per_dev + 1, 3 * LANES, 2 * LANES), jnp.bfloat16),
            pltpu.VMEM((per_dev, tiles // 2, rows, 2 * LANES), jnp.float32),
            pltpu.SMEM((per_dev,), jnp.int32),
            pltpu.SMEM((2, per_dev), jnp.int32),
            pltpu.SemaphoreType.DMA((slots,)),
            pltpu.SemaphoreType.DMA((slots,)),
            pltpu.SemaphoreType.DMA((3,)),
            pltpu.SemaphoreType.REGULAR((2,)),
        ],
        compiler_params=pltpu.CompilerParams(
            collective_id=0, has_side_effects=True, vmem_limit_bytes=40 * 1024 * 1024
        ),
        name="insar_boxes",
    )(*[pltpu.with_memory_space_constraint(operand, pltpu.HBM) for operand in (counts, looks, x)])


def write(ifg, coh, ifg_out, coh_out, sem):
    copies = []
    for a in range(ifg.shape[0]):
        for src, dst in ((ifg, ifg_out), (coh, coh_out)):
            kept = src.at[a, pl.ds(0, MAXP)]
            copies.append(pltpu.make_async_copy(kept, dst.at[a], sem.at[len(copies)]))
    for copy in copies:
        copy.start()
    for copy in copies:
        copy.wait()


def written(ifg, coh):
    shapes = [(v.shape[0], MAXP) + v.shape[2:] for v in (ifg, coh)]
    hbm, vmem = [pl.BlockSpec(memory_space=space) for space in (pltpu.HBM, pltpu.VMEM)]
    return pl.pallas_call(
        write,
        in_specs=[vmem, vmem],
        out_specs=[hbm, hbm],
        out_shape=[jax.ShapeDtypeStruct(shape, jnp.bfloat16) for shape in shapes],
        scratch_shapes=[pltpu.SemaphoreType.DMA((2 * ifg.shape[0],))],
        compiler_params=pltpu.CompilerParams(vmem_limit_bytes=2 * 1024 * 1024),
        name="insar_write",
    )(ifg, coh)


def local(slc_stack, partner_count, look_sizes):
    acq_total = lax.axis_size("tm") * slc_stack.shape[0]
    return tuple(written(*computed(slc_stack, partner_count, look_sizes.T, acq_total)))


def solution(mesh):
    return jax.shard_map(
        local,
        mesh=mesh,
        in_specs=(P("tm", None, "rows", None), P("tm"), P("tm", None)),
        out_specs=(P("tm", None, None, "rows", None), P("tm", None, "rows", None)),
        check_vma=False,
    )
```

time: 21.8 us -> 18.1 us (0.83)
  the two profiles are of different devices: /device:TPU:0 before, /device:TPU:19 now
where the time goes in v1:
time: 18.1 us; the launch traced here: 17.9 us
  Pallas kernels  17.3 us (96%)
  between operations  0.64 us (4%)
    pallas_call x1, Pallas kernels, computed(): pl.pallas_call(functools.partial(kernel, acq_total), in_specs=[hbm, hbm,...  15.8 us
    pallas_call x1, Pallas kernels, written(): pl.pallas_call(write, in_specs=[vmem, vmem], out_specs=[hbm, hbm], out_sh...  1.46 us

profile of v1, /device:TPU:19, one launch (start us, length us, event | category | flops | bytes accessed | tf_op | source)
XLA Modules:
  0.0 17.9 jit_solution(14217601562336835251)
XLA Ops:
  0.6 15.8 %insar_boxes.1 = (bf16[4,7,2,8,2048]{4,3,2,1,0:T(8,128)(2,1)S(1)}, bf16[4,7,8,2048]{3,2,1,0:T(8,128)(2,1)S(1)}) custom-call(s32[4]{0:T(128)} %counts_in.1, s32[2,4]{1,0:T(2,128)} %bitcast.1, bf16[4,2,8,2048]{3,2,1,0:T(8,128)(2,1)} %x.1), custom_call_target="tpu_custom_call" | custom-call | tf_op jit(solution)/shard_map/insar_boxes/pallas_call | solution.py:399
  16.5 1.5 %insar_write.1 = (bf16[4,6,2,8,2048]{4,3,2,1,0:T(8,128)(2,1)}, bf16[4,6,8,2048]{3,2,1,0:T(8,128)(2,1)}) custom-call(bf16[4,7,2,8,2048]{4,3,2,1,0:T(8,128)(2,1)S(1)} %get-tuple-element.4.ifg, bf16[4,7,8,2048]{3,2,1,0:T(8,128)(2,1)S(1)} %get-tuple-element.5.coh), custom_call_target="tpu_custom_call" | custom-call | tf_op jit(solution)/shard_map/insar_write/pallas_call | solution.py:446

commit v2 on v1

--- a/solution.py
+++ b/solution.py
@@ -11,6 +11,7 @@
 MAXP = 6
 HR = 2
 LANES = 128
+LEAD = 8
 
 epsilon = 1e-06
 tiny = 1.2e-38
@@ -44,7 +45,7 @@
 
 def kernel(
     acq_total, counts_in, looks_in, x, ifg, coh,
-    held, planes, power, sums_a, sums_b, lhs_a, lhs_b, bands, own_box, counts, looks,
+    held, planes, power, power_sums, sums, lhs, bands, own_box, counts, looks,
     send_sem, recv_sem, local_sem, ready_sem,
 ):
     tm, line = lax.axis_index("tm"), lax.axis_index("rows")
@@ -69,7 +70,7 @@
 
     barrier = pltpu.get_barrier_semaphore()
     for there, device in [
-        (tm + 1 < tm_count, next_dev),
+        (even & (tm + 1 < tm_count), next_dev),
         (tm + 2 < tm_count, {"tm": tm + 2}),
         (below, down_dev),
     ]:
@@ -78,19 +79,27 @@
         def _():
             pl.semaphore_signal(barrier, inc=1, device_id=device, device_id_type=MESH)
 
-    earlier = sum(jnp.where(there, 1, 0) for there in (tm >= 1, tm >= 2, above))
+    earlier = sum(jnp.where(there, 1, 0) for there in (odd, tm >= 2, above))
 
     @pl.when(earlier > 0)
     def _():
         pl.semaphore_wait(barrier, earlier)
 
-    for index, (there, device) in enumerate([(above, up_dev), (odd, near_dev)]):
-
+    def tell(index, there, device):
         @pl.when(there)
         def _():
             pl.semaphore_signal(
                 ready_sem.at[index], inc=1, device_id=device, device_id_type=MESH
             )
+
+    def told(index, there):
+        @pl.when(there)
+        def _():
+            pl.semaphore_wait(ready_sem.at[index], 1)
+
+    tell(0, above, up_dev)
+    tell(1, odd, near_dev)
+    tell(2, even & (tm >= 2), far_dev)
 
     starts = [per_dev, per_dev + far, 2 * per_dev]
     sizes = [far, per_dev - far, far]
@@ -125,6 +134,12 @@
         dst = held.at[per_dev + k, :, pl.ds(HR, rows - 2 * HR)]
         return copy(src, dst, onward_slot + 2 + k, mid_slot + k, next_dev)
 
+    def onward_halo(side):
+        low = rows + side * HR
+        recv = (down_slot, up_slot)[side]
+        send = onward_slot + 2 + far + side
+        return copy(span(2, low, HR), span(0, low, HR), send, recv, next_dev)
+
     def down(g):
         return copy(span(g, rows - HR, HR), span(g, rows, HR), down_slot + g, down_slot + g, down_dev)
 
@@ -146,6 +161,11 @@
     sends = [odd, tm >= 1, tm >= 2]
     to = [near_dev, near_dev, far_dev]
 
+    line_even = lax.rem(line, 2) == 0
+    far_down, far_up = below & ~line_even, above & line_even
+    goes_down = [below & (even | line_even), below, below]
+    goes_up = [above & (even | ~line_even), above, above]
+
     def when(condition, action):
         @pl.when(condition)
         def _():
@@ -160,10 +180,9 @@
             middle(starts[g] + k, to[g]).start()
 
     when(above, lambda: own_up().start())
-    for g in (2, 0, 1):
-        when(sends[g], lambda: send_edges(g))
-    for g in (2, 0, 1):
-        when(sends[g], lambda: send_middles(g))
+    when(sends[2], lambda: send_edges(2))
+    when(sends[0], lambda: send_edges(0))
+    when(odd, lambda: send_edges(1))
     for local_copy in local_copies:
         local_copy.start()
 
@@ -171,8 +190,8 @@
         def act():
             for side in range(2):
                 edge(g, side, to[g]).wait_recv()
-            when(below, lambda: down(g).start())
-            when(above, lambda: up(g).start())
+            when(goes_down[g], lambda: down(g).start())
+            when(goes_up[g], lambda: up(g).start())
 
         when(has[g], act)
 
@@ -201,12 +220,14 @@
     zero = jnp.zeros((rows, LANES), jnp.float32)
 
     def spread(get, count, out):
-        pieces = [get(t) for t in range(-1, count + 1)]
+        pieces = [get(-1), get(0)]
         for t in range(0, count, 2):
+            pieces += [get(t + 1), get(t + 2)]
             at = slice(t * rows, (t + 2) * rows)
             out[at, :LANES] = pieces[t + 1]
             out[at, LANES : 2 * LANES] = pieces[t + 2]
             out[at, 2 * LANES :] = jnp.where(near_edge, pieces[t + 3], pieces[t])
+            yield
 
     def pair(first, second):
         return jnp.concatenate([first, second], 0).astype(jnp.bfloat16)
@@ -221,21 +242,26 @@
             for r in range(rows):
                 short = pairs[r] + v[r + 3]
                 where = pl.ds(h * rows + r, 8, stride=rows)
-                sums_a[0, where, :] = short
-                sums_a[1, where, :] = short + (v[r] + v[r + 4])
+                power_sums[0, where, :] = short
+                power_sums[1, where, :] = short + (v[r] + v[r + 4])
         for n in range(2):
 
             def tile(t):
-                return sums_a[n, t * rows : (t + 1) * rows, :] if 0 <= t < tiles else zero
-
-            spread(lambda t: pair(tile(t), tile(t + half)), half, power.at[p, n])
+                return power_sums[n, t * rows : (t + 1) * rows, :] if 0 <= t < tiles else zero
+
+            for _ in spread(lambda t: pair(tile(t), tile(t + half)), half, power.at[p, n]):
+                pass
 
     def boxed_power(a, p):
         result = jnp.dot(power[p, jnp.where(looks[0, a] >= HR, 1, 0)], bands[a], preferred_element_type=jnp.float32)
+        return paired(result)
+
+    def paired(result):
         result = result.reshape(half // 2, 2, rows, 2 * LANES)
         return [result[m % (half // 2), m // (half // 2)] for m in range(half)]
 
-    def first_half(a, p, sums, lhs):
+    def first_half(a, p):
+        middle_pair = [None, None]
         outer = jnp.where(looks[0, a] >= HR, 1.0, 0.0).astype(jnp.float32)
         for h in range(0, tiles, 8):
             real, imag = [], []
@@ -244,50 +270,74 @@
                 far_re, far_im = plane(p, 0, r, h), plane(p, 1, r, h)
                 real.append(own_re * far_re + own_im * far_im)
                 imag.append(own_im * far_re - own_re * far_im)
-            for field, v in enumerate((real, imag)):
-                pairs = [v[r] + v[r + 1] for r in range(1, rows + 2)]
-                for r in range(rows):
-                    row_total = pairs[r] + v[r + 3] + (v[r] + v[r + 4]) * outer
-                    sums[field, pl.ds(h * rows + r, 8, stride=rows), :] = row_total
+                if r < 2 * HR:
+                    continue
+                for field, v in enumerate((real, imag)):
+                    first = r - 2 * HR
+                    if first % 2 == 0:
+                        middle_pair[field] = v[first + 2] + v[first + 3]
+                        row_total = v[first + 1] + middle_pair[field]
+                    else:
+                        row_total = middle_pair[field] + v[first + 3]
+                    row_total = row_total + (v[first] + v[first + 4]) * outer
+                    sums[field, pl.ds(h * rows + first, 8, stride=rows), :] = row_total
+                yield
 
         def fields(t):
             if not 0 <= t < tiles:
                 return pair(zero, zero)
             return pair(*[sums[f, t * rows : (t + 1) * rows, :] for f in range(2)])
 
-        spread(fields, tiles, lhs)
+        yield from spread(fields, tiles, lhs)
 
     def store(ref, at, value):
         for side in range(2):
             where = slice(at + side * LANES, at + (side + 1) * LANES)
             ref[:, where] = value[side * rows : (side + 1) * rows]
 
-    def second_half(a, p, lhs):
+    def second_half(a, p):
         j = p - a - 1
         live = (j < counts[a]) & (tm * per_dev + p < acq_total)
-        which = jnp.where(live, a, per_dev)
-        boxed = jnp.dot(lhs[...], bands[which], preferred_element_type=jnp.float32)
-        boxed = boxed.reshape(half, 2, rows, 2 * LANES)
-        other = boxed_power(a, p)
+        shared = power[p, jnp.where(looks[0, a] >= HR, 1, 0)]
+        stacked = jnp.concatenate([lhs[...], shared], 0)
+        boxed = jnp.dot(stacked, bands[a], preferred_element_type=jnp.float32)
+        other = paired(boxed[tiles * rows :])
+        boxed = boxed[: tiles * rows].reshape(half, 2, rows, 2 * LANES)
         area = ((2 * looks[0, a] + 1) * (2 * looks[1, a] + 1)).astype(jnp.float32)
-        scale = 1.0 / jnp.full((rows, 2 * LANES), area, jnp.float32)
+        alive = jnp.where(live, 1.0, 0.0).astype(jnp.float32)
+        scale = alive / jnp.full((rows, 2 * LANES), area, jnp.float32)
+        yield
         for m in range(half):
             re, im = boxed[m, 0], boxed[m, 1]
             size = re * re + im * im
             level = own_box[a, m] * other[m] + epsilon
-            value = size * lax.rsqrt(jnp.maximum(size * level, tiny))
+            value = size * alive * lax.rsqrt(jnp.maximum(size * level, tiny))
             for ref, v in ((ifg.at[a, j, 0], re * scale), (ifg.at[a, j, 1], im * scale), (coh.at[a, j], value)):
                 store(ref, 2 * m * LANES, pair(v[:, :LANES], v[:, LANES:]))
-
-    def slot(a, p, sums, lhs):
-        first_half(a, p, sums, lhs)
-        second_half(a, p, lhs)
-
-    scratch = [(sums_a, lhs_a), (sums_b, lhs_b)]
-
-    def slots(pairs):
-        for n, (a, p) in enumerate(pairs):
-            slot(a, p, *scratch[n % 2])
+            yield
+
+    opened = []
+
+    def step(prologue, following):
+        @pl.when(tm >= 0)
+        def _():
+            closing = second_half(*opened[0]) if opened else iter(())
+            next(closing, None)
+            prologue()
+            opening = first_half(*following) if following else iter(())
+            for _ in itertools.islice(opening, LEAD):
+                pass
+            for _ in closing:
+                for _ in itertools.islice(opening, 2):
+                    pass
+            for _ in opening:
+                pass
+
+        opened[:] = [following] if following else []
+
+    def slots(pairs, prologue=lambda: None):
+        for n, following in enumerate(pairs):
+            step(prologue if n == 0 else lambda: None, following)
 
     for local_copy in local_copies:
         local_copy.wait()
@@ -296,35 +346,47 @@
     across = lax.broadcasted_iota(jnp.int32, (3 * LANES, 2 * LANES), 1)
     source = jnp.where(inner < 2 * LANES + LANES // 2, inner, inner - 3 * LANES)
     distance = jnp.abs(source - across)
-    bands[per_dev] = jnp.zeros((3 * LANES, 2 * LANES), jnp.bfloat16)
 
     @pl.loop(0, per_dev)
     def _(a):
         bands[a] = jnp.where(distance <= looks[1, a], 1.0, 0.0).astype(jnp.bfloat16)
         place(a, 0, rows, None)
 
-    @pl.when(below)
+    told(0, below)
+    when(below, lambda: own_down().start())
+    told(1, even & (tm + 1 < tm_count))
+    told(2, even & (tm + 2 < tm_count))
+    tell(3, even & (tm + 2 < tm_count), {"tm": tm + 2})
+    told(3, even & (tm >= 2))
+    when(even & sends[1], lambda: send_edges(1))
+    when(sends[2], lambda: send_middles(2))
+    when(sends[0], lambda: send_middles(0))
+    when(odd, lambda: send_middles(1))
+
+    own_pairs = [(a, p) for p in range(1, per_dev) for a in range(p)]
+
+    def own_halo():
+        when(above, lambda: own_down().wait_recv())
+        when(below, lambda: own_up().wait_recv())
+
+    def own_work():
+        @pl.loop(0, per_dev)
+        def _(a):
+            place(a, rows, 2 * HR, inside)
+            partner_power(a)
+            box = boxed_power(a, a)
+            for m in range(half):
+                own_box[a, m] = box[m]
+
+        slots(own_pairs)
+        step(lambda: None, None)
+
+    outer_line = (line == 0) | (line == line_count - 1)
+
+    @pl.when(outer_line)
     def _():
-        pl.semaphore_wait(ready_sem.at[0], 1)
-        own_down().start()
-
-    @pl.when(even)
-    def _():
-        pl.semaphore_wait(ready_sem.at[1], 1)
-
-    when(above, lambda: own_down().wait_recv())
-    when(below, lambda: own_up().wait_recv())
-
-    @pl.loop(0, per_dev)
-    def _(a):
-        place(a, rows, 2 * HR, inside)
-        partner_power(a)
-        box = boxed_power(a, a)
-        for m in range(half):
-            own_box[a, m] = box[m]
-
-    own_pairs = [(a, p) for p in range(1, per_dev) for a in range(p)]
-    early, late = own_pairs[: len(own_pairs) // 2], own_pairs[len(own_pairs) // 2 :]
+        own_halo()
+        own_work()
 
     relay(2)
 
@@ -334,9 +396,11 @@
             onward_edge(side).start()
 
     when(even, lambda: relay(0))
-    slots(early)
-    relay(1)
-    slots(late)
+    when(~outer_line, own_halo)
+    when(even & sends[1], lambda: send_middles(1))
+    when(odd, lambda: relay(1))
+    when(~outer_line, own_work)
+    when(even, lambda: relay(1))
 
     @pl.when(has[2])
     def _():
@@ -344,17 +408,20 @@
             middle(2 * per_dev + k, far_dev).wait_recv()
             when(passes, lambda: onward_middle(k).start())
 
-    when(odd, lambda: relay(0))
-
     def partner(p, there, first):
-        place(p, 0, rows, there)
-        place(p, rows, 2 * HR, inside & there)
-        partner_power(p)
-        slots([(a, p) for a in range(first, per_dev)])
+        def prologue():
+            place(p, 0, rows, there)
+            place(p, rows, 2 * HR, inside & there)
+            partner_power(p)
+
+        slots([(a, p) for a in range(first, per_dev)], prologue)
 
     halo(2)
+    when(passes & far_up, lambda: onward_halo(0).start())
+    when(passes & far_down, lambda: onward_halo(1).start())
     for k in range(far):
         partner(2 * per_dev + k, has[2], 2 * per_dev + k - MAXP)
+    when(odd, lambda: relay(0))
 
     def arrived(p):
         g = 0 if p < starts[1] else 1
@@ -367,12 +434,13 @@
         when(even, lambda: arrived(p_even))
         when(odd, lambda: arrived(p_odd))
         partner(jnp.where(odd, p_odd, p_even), has[0], 0)
+    step(lambda: None, None)
 
     when(above, lambda: own_up().wait_send())
     when(below, lambda: own_down().wait_send())
     for g in range(3):
-        when(has[g] & below, lambda: down(g).wait_send())
-        when(has[g] & above, lambda: up(g).wait_send())
+        when(has[g] & goes_down[g], lambda: down(g).wait_send())
+        when(has[g] & goes_up[g], lambda: up(g).wait_send())
 
         @pl.when(sends[g])
         def _():
@@ -387,6 +455,8 @@
             onward_edge(side).wait_send()
         for k in range(far):
             onward_middle(k).wait_send()
+        when(far_up, lambda: onward_halo(0).wait_send())
+        when(far_down, lambda: onward_halo(1).wait_send())
 
 
 def computed(x, counts, looks, acq_total):
@@ -411,15 +481,14 @@
             pltpu.VMEM((2, tiles * rows, LANES), jnp.float32),
             pltpu.VMEM((2, tiles * rows, LANES), jnp.float32),
             pltpu.VMEM((tiles * rows, 3 * LANES), jnp.bfloat16),
-            pltpu.VMEM((tiles * rows, 3 * LANES), jnp.bfloat16),
-            pltpu.VMEM((per_dev + 1, 3 * LANES, 2 * LANES), jnp.bfloat16),
+            pltpu.VMEM((per_dev, 3 * LANES, 2 * LANES), jnp.bfloat16),
             pltpu.VMEM((per_dev, tiles // 2, rows, 2 * LANES), jnp.float32),
             pltpu.SMEM((per_dev,), jnp.int32),
             pltpu.SMEM((2, per_dev), jnp.int32),
             pltpu.SemaphoreType.DMA((slots,)),
             pltpu.SemaphoreType.DMA((slots,)),
             pltpu.SemaphoreType.DMA((3,)),
-            pltpu.SemaphoreType.REGULAR((2,)),
+            pltpu.SemaphoreType.REGULAR((4,)),
         ],
         compiler_params=pltpu.CompilerParams(
             collective_id=0, has_side_effects=True, vmem_limit_bytes=40 * 1024 * 1024

time: 18.1 us -> 16.1 us (0.89)
  Pallas kernels: 17.3 us -> 15.3 us
    pallas_call x1, Pallas kernels: 15.8 us -> 13.8 us  [computed(): pl.pallas_call(functools.partial(kernel, acq_total), in_specs=[hbm, hbm,...]
where the time goes in v2:
time: 16.1 us; the launch traced here: 15.9 us
  Pallas kernels  15.3 us (95%)
  between operations  0.64 us (4%)
    pallas_call x1, Pallas kernels, computed(): pl.pallas_call(functools.partial(kernel, acq_total), in_specs=[hbm, hbm,...  13.8 us
    pallas_call x1, Pallas kernels, written(): pl.pallas_call(write, in_specs=[vmem, vmem], out_specs=[hbm, hbm], out_sh...  1.46 us

profile of v2, /device:TPU:19, one launch (start us, length us, event | category | flops | bytes accessed | tf_op | source)
XLA Modules:
  0.0 15.9 jit_solution(5937488911448720307)
XLA Ops:
  0.6 13.8 %insar_boxes.1 = (bf16[4,7,2,8,2048]{4,3,2,1,0:T(8,128)(2,1)S(1)}, bf16[4,7,8,2048]{3,2,1,0:T(8,128)(2,1)S(1)}) custom-call(s32[4]{0:T(128)} %counts_in.1, s32[2,4]{1,0:T(2,128)} %bitcast.1, bf16[4,2,8,2048]{3,2,1,0:T(8,128)(2,1)} %x.1), custom_call_target="tpu_custom_call" | custom-call | tf_op jit(solution)/shard_map/insar_boxes/pallas_call | solution.py:469
  14.5 1.5 %insar_write.1 = (bf16[4,6,2,8,2048]{4,3,2,1,0:T(8,128)(2,1)}, bf16[4,6,8,2048]{3,2,1,0:T(8,128)(2,1)}) custom-call(bf16[4,7,2,8,2048]{4,3,2,1,0:T(8,128)(2,1)S(1)} %get-tuple-element.4.ifg, bf16[4,7,8,2048]{3,2,1,0:T(8,128)(2,1)S(1)} %get-tuple-element.5.coh), custom_call_target="tpu_custom_call" | custom-call | tf_op jit(solution)/shard_map/insar_write/pallas_call | solution.py:515

commit v3 on v2

--- a/solution.py
+++ b/solution.py
@@ -408,19 +408,24 @@
             middle(2 * per_dev + k, far_dev).wait_recv()
             when(passes, lambda: onward_middle(k).start())
 
-    def partner(p, there, first):
+    def partners(chosen, there, placed=False):
         def prologue():
-            place(p, 0, rows, there)
-            place(p, rows, 2 * HR, inside & there)
-            partner_power(p)
-
-        slots([(a, p) for a in range(first, per_dev)], prologue)
-
+            for p, _ in chosen:
+                if not placed:
+                    place(p, 0, rows, there)
+                place(p, rows, 2 * HR, inside & there)
+            for p, _ in chosen:
+                partner_power(p)
+
+        slots([(a, p) for p, first in chosen for a in range(first, per_dev)], prologue)
+
+    ends = [2 * per_dev + k for k in range(far)]
+    for p in ends:
+        place(p, 0, rows, has[2])
     halo(2)
     when(passes & far_up, lambda: onward_halo(0).start())
     when(passes & far_down, lambda: onward_halo(1).start())
-    for k in range(far):
-        partner(2 * per_dev + k, has[2], 2 * per_dev + k - MAXP)
+    partners([(p, p - MAXP) for p in ends], has[2], placed=True)
     when(odd, lambda: relay(0))
 
     def arrived(p):
@@ -429,11 +434,17 @@
         if p == starts[g]:
             halo(g)
 
+    def arrive(group):
+        for p in group:
+            arrived(p)
+
     turns = list(range(starts[0], starts[2]))
-    for p_even, p_odd in zip(turns, turns[far:] + turns[:far]):
-        when(even, lambda: arrived(p_even))
-        when(odd, lambda: arrived(p_odd))
-        partner(jnp.where(odd, p_odd, p_even), has[0], 0)
+    swapped = turns[far:] + turns[:far]
+    for n in range(0, per_dev, 2):
+        when(even, lambda: arrive(turns[n : n + 2]))
+        when(odd, lambda: arrive(swapped[n : n + 2]))
+        both = zip(turns[n : n + 2], swapped[n : n + 2])
+        partners([(jnp.where(odd, p_odd, p_even), 0) for p_even, p_odd in both], has[0])
     step(lambda: None, None)
 
     when(above, lambda: own_up().wait_send())

time: 16.1 us -> 16 us (level)
  no operation moved by 1% of the time
where the time goes in v3:
time: 16 us; the launch traced here: 15.8 us
  Pallas kernels  15.2 us (95%)
  between operations  0.64 us (4%)
    pallas_call x1, Pallas kernels, computed(): pl.pallas_call(functools.partial(kernel, acq_total), in_specs=[hbm, hbm,...  13.7 us
    pallas_call x1, Pallas kernels, written(): pl.pallas_call(write, in_specs=[vmem, vmem], out_specs=[hbm, hbm], out_sh...  1.46 us

profile of v3, /device:TPU:19, one launch (start us, length us, event | category | flops | bytes accessed | tf_op | source)
XLA Modules:
  0.0 15.8 jit_solution(2263293250419672045)
XLA Ops:
  0.6 13.7 %insar_boxes.1 = (bf16[4,7,2,8,2048]{4,3,2,1,0:T(8,128)(2,1)S(1)}, bf16[4,7,8,2048]{3,2,1,0:T(8,128)(2,1)S(1)}) custom-call(s32[4]{0:T(128)} %counts_in.1, s32[2,4]{1,0:T(2,128)} %bitcast.1, bf16[4,2,8,2048]{3,2,1,0:T(8,128)(2,1)} %x.1), custom_call_target="tpu_custom_call" | custom-call | tf_op jit(solution)/shard_map/insar_boxes/pallas_call | solution.py:480
  14.3 1.5 %insar_write.1 = (bf16[4,6,2,8,2048]{4,3,2,1,0:T(8,128)(2,1)}, bf16[4,6,8,2048]{3,2,1,0:T(8,128)(2,1)}) custom-call(bf16[4,7,2,8,2048]{4,3,2,1,0:T(8,128)(2,1)S(1)} %get-tuple-element.4.ifg, bf16[4,7,8,2048]{3,2,1,0:T(8,128)(2,1)S(1)} %get-tuple-element.5.coh), custom_call_target="tpu_custom_call" | custom-call | tf_op jit(solution)/shard_map/insar_write/pallas_call | solution.py:526

commit v4 on v3

--- a/solution.py
+++ b/solution.py
@@ -43,9 +43,196 @@
         self.over().wait_recv()
 
 
+class Slots:
+    def __init__(
+        self, tm, line, acq_total, dims, planes, power_sums, sums, lhs, bands, own_box, counts, looks
+    ):
+        self.tm, self.acq_total, self.dims = tm, acq_total, dims
+        self.planes, self.power_sums, self.sums, self.lhs = planes, power_sums, sums, lhs
+        self.bands, self.own_box, self.counts, self.looks = bands, own_box, counts, looks
+        rows = dims[1]
+        self.tiles = dims[2] // LANES
+        side_row = lax.broadcasted_iota(jnp.int32, (2 * HR, LANES), 0)
+        above, below = line >= 1, line + 1 < lax.axis_size("rows")
+        self.inside = ((side_row < HR) & above) | ((side_row >= HR) & below)
+        self.near_edge = lax.broadcasted_iota(jnp.int32, (2 * rows, LANES), 1) < LANES // 2
+        self.zero = jnp.zeros((rows, LANES), jnp.float32)
+        self.order = [rows + k for k in range(HR)] + list(range(rows))
+        self.order += [rows + HR + k for k in range(HR)]
+        self.opened = []
+
+    def place(self, src, dst, first, count, keep):
+        for part in range(2):
+            for t in range(self.tiles):
+                v = src[part, first : first + count, t * LANES : (t + 1) * LANES]
+                v = v.astype(jnp.float32)
+                if keep is not None:
+                    v = jnp.where(keep, v, 0.0)
+                dst[part, pl.ds(first * self.tiles + t, count, stride=self.tiles), :] = v
+
+    def plane(self, ref, part, r, h):
+        at = self.order[r] * self.tiles + h
+        return ref[part, at : at + 8, :]
+
+    def spread(self, get, count, out):
+        rows = self.dims[1]
+        pieces = [get(-1), get(0)]
+        for t in range(0, count, 2):
+            pieces += [get(t + 1), get(t + 2)]
+            at = slice(t * rows, (t + 2) * rows)
+            out[at, :LANES] = pieces[t + 1]
+            out[at, LANES : 2 * LANES] = pieces[t + 2]
+            out[at, 2 * LANES :] = jnp.where(self.near_edge, pieces[t + 3], pieces[t])
+            yield
+
+    def partner_power(self, ref, out):
+        rows, tiles = self.dims[1], self.tiles
+        half = tiles // 2
+        for h in range(0, tiles, 8):
+            v = []
+            for r in range(rows + 2 * HR):
+                re, im = self.plane(ref, 0, r, h), self.plane(ref, 1, r, h)
+                v.append(re * re + im * im)
+            pairs = [v[r] + v[r + 1] for r in range(1, rows + 2)]
+            for r in range(rows):
+                short = pairs[r] + v[r + 3]
+                where = pl.ds(h * rows + r, 8, stride=rows)
+                self.power_sums[0, where, :] = short
+                self.power_sums[1, where, :] = short + (v[r] + v[r + 4])
+        for n in range(2):
+
+            def tile(t):
+                inside = 0 <= t < tiles
+                return self.power_sums[n, t * rows : (t + 1) * rows, :] if inside else self.zero
+
+            for _ in self.spread(lambda t: pair(tile(t), tile(t + half)), half, out.at[n]):
+                pass
+
+    def outer(self, a):
+        return jnp.where(self.looks[0, a] >= HR, 1.0, 0.0).astype(jnp.float32)
+
+    def factors(self, a, p):
+        per_dev, rows, _ = self.dims
+        live = (p - a - 1 < self.counts[a]) & (self.tm * per_dev + p < self.acq_total)
+        area = ((2 * self.looks[0, a] + 1) * (2 * self.looks[1, a] + 1)).astype(jnp.float32)
+        alive = jnp.where(live, 1.0, 0.0).astype(jnp.float32)
+        return alive, alive / jnp.full((rows, LANES), area, jnp.float32)
+
+    def chosen(self, a, power):
+        return power[jnp.where(self.looks[0, a] >= HR, 1, 0)]
+
+    def paired(self, result):
+        quarter = self.tiles // 4
+        result = result.reshape(quarter, 2, self.dims[1], 2 * LANES)
+        return [result[m % quarter, m // quarter] for m in range(2 * quarter)]
+
+    def boxed_power(self, a, power):
+        result = jnp.dot(
+            self.chosen(a, power), self.bands[a], preferred_element_type=jnp.float32
+        )
+        return self.paired(result)
+
+    def first_half(self, a, far):
+        rows, tiles, own = self.dims[1], self.tiles, self.planes.at[a]
+        middle_pair = [None, None]
+        outer = self.outer(a)
+        for h in range(0, tiles, 8):
+            real, imag = [], []
+            for r in range(rows + 2 * HR):
+                own_re, own_im = self.plane(own, 0, r, h), self.plane(own, 1, r, h)
+                far_re, far_im = self.plane(far, 0, r, h), self.plane(far, 1, r, h)
+                real.append(own_re * far_re + own_im * far_im)
+                imag.append(own_im * far_re - own_re * far_im)
+                if r < 2 * HR:
+                    continue
+                for field, v in enumerate((real, imag)):
+                    first = r - 2 * HR
+                    if first % 2 == 0:
+                        middle_pair[field] = v[first + 2] + v[first + 3]
+                        row_total = v[first + 1] + middle_pair[field]
+                    else:
+                        row_total = middle_pair[field] + v[first + 3]
+                    row_total = row_total + (v[first] + v[first + 4]) * outer
+                    self.sums[field, pl.ds(h * rows + first, 8, stride=rows), :] = row_total
+                yield
+
+        def fields(t):
+            if not 0 <= t < tiles:
+                return pair(self.zero, self.zero)
+            return pair(*[self.sums[f, t * rows : (t + 1) * rows, :] for f in range(2)])
+
+        yield from self.spread(fields, tiles, self.lhs)
+
+    def store(self, ref, at, value):
+        rows = self.dims[1]
+        for side in range(2):
+            where = slice(at + side * LANES, at + (side + 1) * LANES)
+            ref[:, where] = value[side * rows : (side + 1) * rows]
+
+    def second_half(self, a, p, power, ifg, coh):
+        rows, half = self.dims[1], self.tiles // 2
+        stacked = jnp.concatenate([self.lhs[...], self.chosen(a, power)], 0)
+        boxed = jnp.dot(stacked, self.bands[a], preferred_element_type=jnp.float32)
+        other = self.paired(boxed[self.tiles * rows :])
+        boxed = boxed[: self.tiles * rows].reshape(half, 2, rows, 2 * LANES)
+        alive, scale = self.factors(a, p)
+        scale = jnp.concatenate([scale, scale], 1)
+        if alive.ndim:
+            alive = jnp.concatenate([alive, alive], 1)
+        yield
+        for m in range(half):
+            re, im = boxed[m, 0], boxed[m, 1]
+            size = re * re + im * im
+            level = self.own_box[a, m] * other[m] + epsilon
+            value = size * alive * lax.rsqrt(jnp.maximum(size * level, tiny))
+            for ref, v in ((ifg.at[0], re * scale), (ifg.at[1], im * scale), (coh, value)):
+                self.store(ref, 2 * m * LANES, pair(v[:, :LANES], v[:, LANES:]))
+            yield
+
+    def step(self, following, prologue=lambda: None):
+        closing = iter(())
+        if self.opened:
+            a, p, _, power, ifg, coh = self.opened.pop()
+            closing = self.second_half(a, p, power, ifg, coh)
+        next(closing, None)
+        prologue()
+        opening = iter(())
+        if following is not None:
+            opening = self.first_half(following[0], following[2])
+            self.opened.append(following)
+        for _ in itertools.islice(opening, LEAD):
+            pass
+        for _ in closing:
+            for _ in itertools.islice(opening, 2):
+                pass
+        for _ in opening:
+            pass
+
+    def slots(self, lanes, prologue=lambda: None):
+        for n, following in enumerate(lanes):
+            self.step(following, prologue if n == 0 else lambda: None)
+
+
+class LateSlots(Slots):
+    def outer(self, a):
+        return self.counts[a, 0]
+
+    def factors(self, a, k):
+        return self.counts[a, 1 + k], self.counts[a, 3 + k]
+
+    def chosen(self, a, power):
+        wide = self.outer(a)[:1] > 0.5
+        wide = jnp.broadcast_to(jnp.concatenate([wide] * 3, 1), power.shape[1:])
+        return jnp.where(wide, power[1], power[0])
+
+
+def pair(first, second):
+    return jnp.concatenate([first, second], 0).astype(jnp.bfloat16)
+
+
 def kernel(
-    acq_total, counts_in, looks_in, x, ifg, coh,
-    held, planes, power, power_sums, sums, lhs, bands, own_box, counts, looks,
+    acq_total, counts_in, looks_in, x, ifg, coh, held, planes, bands, own_box, factors,
+    power, power_sums, sums, lhs, counts, looks,
     send_sem, recv_sem, local_sem, ready_sem,
 ):
     tm, line = lax.axis_index("tm"), lax.axis_index("rows")
@@ -199,145 +386,17 @@
         when(has[g] & below, lambda: up(g).wait_recv())
         when(has[g] & above, lambda: down(g).wait_recv())
 
+    work = Slots(
+        tm, line, acq_total, (per_dev, rows, cols), planes, power_sums, sums, lhs, bands, own_box,
+        counts, looks,
+    )
+    inside = work.inside
+
+    def lane(a, p):
+        return a, p, planes.at[p], power.at[p], ifg.at[a, p - a - 1], coh.at[a, p - a - 1]
+
     def place(p, first, count, keep):
-        for part in range(2):
-            for t in range(tiles):
-                lanes = slice(t * LANES, (t + 1) * LANES)
-                v = held[p, part, first : first + count, lanes].astype(jnp.float32)
-                if keep is not None:
-                    v = jnp.where(keep, v, 0.0)
-                planes[p, part, pl.ds(first * tiles + t, count, stride=tiles), :] = v
-
-    order = [rows + k for k in range(HR)] + list(range(rows)) + [rows + HR + k for k in range(HR)]
-
-    def plane(p, part, r, h):
-        at = order[r] * tiles + h
-        return planes[p, part, at : at + 8, :]
-
-    side_row = lax.broadcasted_iota(jnp.int32, (2 * HR, LANES), 0)
-    inside = ((side_row < HR) & above) | ((side_row >= HR) & below)
-    near_edge = lax.broadcasted_iota(jnp.int32, (2 * rows, LANES), 1) < LANES // 2
-    zero = jnp.zeros((rows, LANES), jnp.float32)
-
-    def spread(get, count, out):
-        pieces = [get(-1), get(0)]
-        for t in range(0, count, 2):
-            pieces += [get(t + 1), get(t + 2)]
-            at = slice(t * rows, (t + 2) * rows)
-            out[at, :LANES] = pieces[t + 1]
-            out[at, LANES : 2 * LANES] = pieces[t + 2]
-            out[at, 2 * LANES :] = jnp.where(near_edge, pieces[t + 3], pieces[t])
-            yield
-
-    def pair(first, second):
-        return jnp.concatenate([first, second], 0).astype(jnp.bfloat16)
-
-    def partner_power(p):
-        for h in range(0, tiles, 8):
-            v = []
-            for r in range(ext_rows):
-                re, im = plane(p, 0, r, h), plane(p, 1, r, h)
-                v.append(re * re + im * im)
-            pairs = [v[r] + v[r + 1] for r in range(1, rows + 2)]
-            for r in range(rows):
-                short = pairs[r] + v[r + 3]
-                where = pl.ds(h * rows + r, 8, stride=rows)
-                power_sums[0, where, :] = short
-                power_sums[1, where, :] = short + (v[r] + v[r + 4])
-        for n in range(2):
-
-            def tile(t):
-                return power_sums[n, t * rows : (t + 1) * rows, :] if 0 <= t < tiles else zero
-
-            for _ in spread(lambda t: pair(tile(t), tile(t + half)), half, power.at[p, n]):
-                pass
-
-    def boxed_power(a, p):
-        result = jnp.dot(power[p, jnp.where(looks[0, a] >= HR, 1, 0)], bands[a], preferred_element_type=jnp.float32)
-        return paired(result)
-
-    def paired(result):
-        result = result.reshape(half // 2, 2, rows, 2 * LANES)
-        return [result[m % (half // 2), m // (half // 2)] for m in range(half)]
-
-    def first_half(a, p):
-        middle_pair = [None, None]
-        outer = jnp.where(looks[0, a] >= HR, 1.0, 0.0).astype(jnp.float32)
-        for h in range(0, tiles, 8):
-            real, imag = [], []
-            for r in range(ext_rows):
-                own_re, own_im = plane(a, 0, r, h), plane(a, 1, r, h)
-                far_re, far_im = plane(p, 0, r, h), plane(p, 1, r, h)
-                real.append(own_re * far_re + own_im * far_im)
-                imag.append(own_im * far_re - own_re * far_im)
-                if r < 2 * HR:
-                    continue
-                for field, v in enumerate((real, imag)):
-                    first = r - 2 * HR
-                    if first % 2 == 0:
-                        middle_pair[field] = v[first + 2] + v[first + 3]
-                        row_total = v[first + 1] + middle_pair[field]
-                    else:
-                        row_total = middle_pair[field] + v[first + 3]
-                    row_total = row_total + (v[first] + v[first + 4]) * outer
-                    sums[field, pl.ds(h * rows + first, 8, stride=rows), :] = row_total
-                yield
-
-        def fields(t):
-            if not 0 <= t < tiles:
-                return pair(zero, zero)
-            return pair(*[sums[f, t * rows : (t + 1) * rows, :] for f in range(2)])
-
-        yield from spread(fields, tiles, lhs)
-
-    def store(ref, at, value):
-        for side in range(2):
-            where = slice(at + side * LANES, at + (side + 1) * LANES)
-            ref[:, where] = value[side * rows : (side + 1) * rows]
-
-    def second_half(a, p):
-        j = p - a - 1
-        live = (j < counts[a]) & (tm * per_dev + p < acq_total)
-        shared = power[p, jnp.where(looks[0, a] >= HR, 1, 0)]
-        stacked = jnp.concatenate([lhs[...], shared], 0)
-        boxed = jnp.dot(stacked, bands[a], preferred_element_type=jnp.float32)
-        other = paired(boxed[tiles * rows :])
-        boxed = boxed[: tiles * rows].reshape(half, 2, rows, 2 * LANES)
-        area = ((2 * looks[0, a] + 1) * (2 * looks[1, a] + 1)).astype(jnp.float32)
-        alive = jnp.where(live, 1.0, 0.0).astype(jnp.float32)
-        scale = alive / jnp.full((rows, 2 * LANES), area, jnp.float32)
-        yield
-        for m in range(half):
-            re, im = boxed[m, 0], boxed[m, 1]
-            size = re * re + im * im
-            level = own_box[a, m] * other[m] + epsilon
-            value = size * alive * lax.rsqrt(jnp.maximum(size * level, tiny))
-            for ref, v in ((ifg.at[a, j, 0], re * scale), (ifg.at[a, j, 1], im * scale), (coh.at[a, j], value)):
-                store(ref, 2 * m * LANES, pair(v[:, :LANES], v[:, LANES:]))
-            yield
-
-    opened = []
-
-    def step(prologue, following):
-        @pl.when(tm >= 0)
-        def _():
-            closing = second_half(*opened[0]) if opened else iter(())
-            next(closing, None)
-            prologue()
-            opening = first_half(*following) if following else iter(())
-            for _ in itertools.islice(opening, LEAD):
-                pass
-            for _ in closing:
-                for _ in itertools.islice(opening, 2):
-                    pass
-            for _ in opening:
-                pass
-
-        opened[:] = [following] if following else []
-
-    def slots(pairs, prologue=lambda: None):
-        for n, following in enumerate(pairs):
-            step(prologue if n == 0 else lambda: None, following)
+        work.place(held.at[p], planes.at[p], first, count, keep)
 
     for local_copy in local_copies:
         local_copy.wait()
@@ -350,6 +409,12 @@
     @pl.loop(0, per_dev)
     def _(a):
         bands[a] = jnp.where(distance <= looks[1, a], 1.0, 0.0).astype(jnp.bfloat16)
+        late = jnp.where(odd, last_partners(per_dev)[1], last_partners(per_dev)[0])
+        factors[a, 0] = jnp.full((rows, LANES), work.outer(a), jnp.float32)
+        for k in range(2):
+            alive, scale = work.factors(a, late + k)
+            factors[a, 1 + k] = jnp.full((rows, LANES), alive, jnp.float32)
+            factors[a, 3 + k] = scale
         place(a, 0, rows, None)
 
     told(0, below)
@@ -373,13 +438,13 @@
         @pl.loop(0, per_dev)
         def _(a):
             place(a, rows, 2 * HR, inside)
-            partner_power(a)
-            box = boxed_power(a, a)
+            work.partner_power(planes.at[a], power.at[a])
+            box = work.boxed_power(a, power.at[a])
             for m in range(half):
                 own_box[a, m] = box[m]
 
-        slots(own_pairs)
-        step(lambda: None, None)
+        work.slots([lane(a, p) for a, p in own_pairs])
+        work.step(None)
 
     outer_line = (line == 0) | (line == line_count - 1)
 
@@ -415,9 +480,10 @@
                     place(p, 0, rows, there)
                 place(p, rows, 2 * HR, inside & there)
             for p, _ in chosen:
-                partner_power(p)
-
-        slots([(a, p) for p, first in chosen for a in range(first, per_dev)], prologue)
+                work.partner_power(planes.at[p], power.at[p])
+
+        chosen_lanes = [lane(a, p) for p, first in chosen for a in range(first, per_dev)]
+        work.slots(chosen_lanes, prologue)
 
     ends = [2 * per_dev + k for k in range(far)]
     for p in ends:
@@ -438,14 +504,14 @@
         for p in group:
             arrived(p)
 
-    turns = list(range(starts[0], starts[2]))
-    swapped = turns[far:] + turns[:far]
+    turns, swapped = turn_order(per_dev)
     for n in range(0, per_dev, 2):
         when(even, lambda: arrive(turns[n : n + 2]))
         when(odd, lambda: arrive(swapped[n : n + 2]))
         both = zip(turns[n : n + 2], swapped[n : n + 2])
-        partners([(jnp.where(odd, p_odd, p_even), 0) for p_even, p_odd in both], has[0])
-    step(lambda: None, None)
+        if n + 2 < per_dev:
+            partners([(jnp.where(odd, p_odd, p_even), 0) for p_even, p_odd in both], has[0])
+    work.step(None)
 
     when(above, lambda: own_up().wait_send())
     when(below, lambda: own_down().wait_send())
@@ -480,20 +546,21 @@
     return pl.pallas_call(
         functools.partial(kernel, acq_total),
         in_specs=[hbm, hbm, hbm],
-        out_specs=[vmem, vmem],
+        out_specs=[vmem] * 7,
         out_shape=[
             jax.ShapeDtypeStruct((per_dev, MAXP + spare, 2, rows, cols), jnp.bfloat16),
             jax.ShapeDtypeStruct((per_dev, MAXP + spare, rows, cols), jnp.bfloat16),
+            jax.ShapeDtypeStruct((total, parts, 2 * rows, cols), x.dtype),
+            jax.ShapeDtypeStruct((total, parts, ext_rows * tiles, LANES), jnp.float32),
+            jax.ShapeDtypeStruct((per_dev, 3 * LANES, 2 * LANES), jnp.bfloat16),
+            jax.ShapeDtypeStruct((per_dev, tiles // 2, rows, 2 * LANES), jnp.float32),
+            jax.ShapeDtypeStruct((per_dev, 5, rows, LANES), jnp.float32),
         ],
         scratch_shapes=[
-            pltpu.VMEM((total, parts, 2 * rows, cols), x.dtype),
-            pltpu.VMEM((total, parts, ext_rows * tiles, LANES), jnp.float32),
             pltpu.VMEM((total, 2, tiles // 2 * rows, 3 * LANES), jnp.bfloat16),
             pltpu.VMEM((2, tiles * rows, LANES), jnp.float32),
             pltpu.VMEM((2, tiles * rows, LANES), jnp.float32),
             pltpu.VMEM((tiles * rows, 3 * LANES), jnp.bfloat16),
-            pltpu.VMEM((per_dev, 3 * LANES, 2 * LANES), jnp.bfloat16),
-            pltpu.VMEM((per_dev, tiles // 2, rows, 2 * LANES), jnp.float32),
             pltpu.SMEM((per_dev,), jnp.int32),
             pltpu.SMEM((2, per_dev), jnp.int32),
             pltpu.SemaphoreType.DMA((slots,)),
@@ -508,35 +575,106 @@
     )(*[pltpu.with_memory_space_constraint(operand, pltpu.HBM) for operand in (counts, looks, x)])
 
 
-def write(ifg, coh, ifg_out, coh_out, sem):
-    copies = []
-    for a in range(ifg.shape[0]):
-        for src, dst in ((ifg, ifg_out), (coh, coh_out)):
-            kept = src.at[a, pl.ds(0, MAXP)]
-            copies.append(pltpu.make_async_copy(kept, dst.at[a], sem.at[len(copies)]))
-    for copy in copies:
-        copy.start()
-    for copy in copies:
-        copy.wait()
-
-
-def written(ifg, coh):
-    shapes = [(v.shape[0], MAXP) + v.shape[2:] for v in (ifg, coh)]
+def write(
+    acq_total, ifg, coh, held, planes, bands, own_box, factors, ifg_out, coh_out,
+    late_ifg, late_coh, late_planes, power, power_sums, sums, lhs, sem,
+):
+    tm, line = lax.axis_index("tm"), lax.axis_index("rows")
+    per_dev, _, _, rows, cols = ifg.shape
+    even, odd = lax.rem(tm, 2) == 0, lax.rem(tm, 2) == 1
+    starts = last_partners(per_dev)
+
+    def copies(start, a, late):
+        low, high = start - a - 1, min(start - a + 1, MAXP)
+        found = []
+        for n, (src, kept, dst) in enumerate(((ifg, late_ifg, ifg_out), (coh, late_coh, coh_out))):
+            slot = 6 * a + 3 * n
+            if late:
+                piece = kept.at[a, pl.ds(0, high - low)]
+                found.append((piece, dst.at[a, pl.ds(low, high - low)], slot))
+                continue
+            for k, (first, end) in enumerate(((0, low), (high, MAXP))):
+                if first < end:
+                    span = pl.ds(first, end - first)
+                    found.append((src.at[a, span], dst.at[a, span], slot + 1 + k))
+        return [pltpu.make_async_copy(src, dst, sem.at[slot]) for src, dst, slot in found]
+
+    def each(act, late, which):
+        for there, start in zip((even, odd), starts):
+
+            @pl.when(there)
+            def _():
+                for a in which:
+                    for copy in copies(start, a, late):
+                        act(copy)
+
+    each(lambda copy: copy.start(), False, range(per_dev))
+    work = LateSlots(
+        tm, line, acq_total, (per_dev, rows, cols), planes, power_sums, sums, lhs, bands, own_box,
+        factors, None,
+    )
+    there = tm + 1 < lax.axis_size("tm")
+    first = jnp.where(odd, starts[1], starts[0])
+    for k in range(2):
+        work.place(held.at[first + k], late_planes.at[k], 0, rows, there)
+        work.place(held.at[first + k], late_planes.at[k], rows, 2 * HR, work.inside & there)
+        work.partner_power(late_planes.at[k], power.at[k])
+    for a in range(per_dev):
+        for k in range(2):
+            work.step(
+                (a, k, late_planes.at[k], power.at[k], late_ifg.at[a, k], late_coh.at[a, k])
+            )
+            if a > 0 and k == 0:
+                each(lambda copy: copy.start(), True, [a - 1])
+    work.step(None)
+    each(lambda copy: copy.start(), True, [per_dev - 1])
+    each(lambda copy: copy.wait(), False, range(per_dev))
+    each(lambda copy: copy.wait(), True, range(per_dev))
+
+
+def turn_order(per_dev):
+    far = MAXP - per_dev
+    turns = list(range(per_dev, 2 * per_dev))
+    return turns, turns[far:] + turns[:far]
+
+
+def last_partners(per_dev):
+    turns, swapped = turn_order(per_dev)
+    return turns[-2], swapped[-2]
+
+
+def written(acq_total, ifg, coh, held, planes, bands, own_box, factors):
+    per_dev, _, _, rows, cols = ifg.shape
+    tiles, ext_rows = cols // LANES, rows + 2 * HR
     hbm, vmem = [pl.BlockSpec(memory_space=space) for space in (pltpu.HBM, pltpu.VMEM)]
     return pl.pallas_call(
-        write,
-        in_specs=[vmem, vmem],
+        functools.partial(write, acq_total),
+        in_specs=[vmem] * 7,
         out_specs=[hbm, hbm],
-        out_shape=[jax.ShapeDtypeStruct(shape, jnp.bfloat16) for shape in shapes],
-        scratch_shapes=[pltpu.SemaphoreType.DMA((2 * ifg.shape[0],))],
-        compiler_params=pltpu.CompilerParams(vmem_limit_bytes=2 * 1024 * 1024),
+        out_shape=[
+            jax.ShapeDtypeStruct((per_dev, MAXP, 2, rows, cols), jnp.bfloat16),
+            jax.ShapeDtypeStruct((per_dev, MAXP, rows, cols), jnp.bfloat16),
+        ],
+        scratch_shapes=[
+            pltpu.VMEM((per_dev, 2, 2, rows, cols), jnp.bfloat16),
+            pltpu.VMEM((per_dev, 2, rows, cols), jnp.bfloat16),
+            pltpu.VMEM((2, 2, ext_rows * tiles, LANES), jnp.float32),
+            pltpu.VMEM((2, 2, tiles // 2 * rows, 3 * LANES), jnp.bfloat16),
+            pltpu.VMEM((2, tiles * rows, LANES), jnp.float32),
+            pltpu.VMEM((2, tiles * rows, LANES), jnp.float32),
+            pltpu.VMEM((tiles * rows, 3 * LANES), jnp.bfloat16),
+            pltpu.SemaphoreType.DMA((6 * per_dev,)),
+        ],
+        compiler_params=pltpu.CompilerParams(vmem_limit_bytes=12 * 1024 * 1024),
         name="insar_write",
-    )(ifg, coh)
+    )(ifg, coh, held, planes, bands, own_box, factors)
 
 
 def local(slc_stack, partner_count, look_sizes):
     acq_total = lax.axis_size("tm") * slc_stack.shape[0]
-    return tuple(written(*computed(slc_stack, partner_count, look_sizes.T, acq_total)))
+    looks = look_sizes.T
+    found = computed(slc_stack, partner_count, looks, acq_total)
+    return tuple(written(acq_total, *found))
 
 
 def solution(mesh):

time: 16 us -> 15.7 us (0.981)
  Pallas kernels: 15.2 us -> 14.9 us
    pallas_call x1, Pallas kernels: 13.7 us -> 12.8 us  [computed(): pl.pallas_call(functools.partial(kernel, acq_total), in_specs=[hbm, hbm,...]
    pallas_call x1, Pallas kernels: 1.46 us -> 2.13 us  [written(): pl.pallas_call(functools.partial(write, acq_total), in_specs=[vmem] * 7,...]
where the time goes in v4:
time: 15.7 us; the launch traced here: 15.5 us
  Pallas kernels  14.9 us (95%)
  between operations  0.64 us (4%)
    pallas_call x1, Pallas kernels, computed(): pl.pallas_call(functools.partial(kernel, acq_total), in_specs=[hbm, hbm,...  12.8 us
    pallas_call x1, Pallas kernels, written(): pl.pallas_call(functools.partial(write, acq_total), in_specs=[vmem] * 7,...  2.13 us

profile of v4, /device:TPU:19, one launch (start us, length us, event | category | flops | bytes accessed | tf_op | source)
XLA Modules:
  0.0 15.5 jit_solution(7143688575486179657)
XLA Ops:
  0.6 12.8 %insar_boxes.1 = (bf16[4,7,2,8,2048]{4,3,2,1,0:T(8,128)(2,1)S(1)}, bf16[4,7,8,2048]{3,2,1,0:T(8,128)(2,1)S(1)}, bf16[10,2,16,2048]{3,2,1,0:T(8,128)(2,1)S(1)}, f...) custom-call(s32[4]{0:T(128)} %counts_in.1, ...), custom_call_target="tpu_custom_call" | custom-call | tf_op jit(solution)/shard_map/insar_boxes/pallas_call | solution.py:546
  13.4 2.1 %insar_write.1 = (bf16[4,6,2,8,2048]{4,3,2,1,0:T(8,128)(2,1)}, bf16[4,6,8,2048]{3,2,1,0:T(8,128)(2,1)}) custom-call(bf16[4,7,2,8,2048]{4,3,2,1,0:T(8,128)(2,1)S(1)} %get-tuple-element.9.ifg, bf16[4,7,8,2048]{3,2,1,0:T(8,128)(2,1)S(1)} %get-tuple-element.10.coh, bf16[10,2,16,2048]{3,2,1,0:T(8,128)(2,1)S(1)} %get-tuple-element.11.held, ...), custom_call_target="tpu_custom_call" | custom-call | tf_op jit(solution)/shard_map/insar_write/pallas_call | solution.py:650
